TPU v7x, 32 devices: a whole 2x2x4 slice. The times are simulated.
32 devices in a mesh: rep: 8 (over z, y), zero: 4 (over x, core).
Axes of the slice: x: 2, y: 2, z: 4, core: 2. Of those that a mesh axis runs over, the one named last changes fastest.
Arguments:
- tokens: bfloat16 [12288, 1280], P(('rep', 'zero')), may hold values from -6 to 6
- cotangent: bfloat16 [12288, 1280], P(('rep', 'zero')), may hold values from -6 to 6
- weights: bfloat16 [1280, 6, 1280], P('zero')
- vectors: bfloat16 [5, 1280], P(None, 'zero')
- error: float32 [10240, 6, 1280], P(('rep', 'zero'))
- previous_right_factors: float32 [6, 1280, 32], P(None, None, 'zero'), may hold values from -6 to 6
- momentum: float32 [1280, 6, 1280], P('zero', None, 'rep')
- vec_momentum: float32 [5, 1280], P(None, 'zero')
- prompt_len: int32 [8], P('rep'), may hold values from 512 to 1024, as said below
Outputs:
- result: bfloat16 [12288, 1280], P(('rep', 'zero'))
- grad_tokens: float32 [12288, 1280], P(('rep', 'zero'))
- grad_weights: float32 [1280, 6, 1280], P('zero', None, 'rep')
- grad_vectors: float32 [5, 1280], P(None, 'zero')
- new_error: float32 [10240, 6, 1280], P(('rep', 'zero'))
- fresh_right_factors: float32 [6, 1280, 32], P(None, None, 'zero')
- new_momentum: float32 [1280, 6, 1280], P('zero', None, 'rep')
- new_vec_momentum: float32 [5, 1280], P(None, 'zero')
- update_weights: float32 [1280, 6, 1280], P('zero', None, 'rep')
- update_vectors: float32 [5, 1280], P(None, 'zero')
Inputs may be any that keep to these rules, and one draw needn't show every extreme that they name: `prompt_len`: valid prompt rows of a group; the other prompt rows of its 1024 are padding.
All inputs are finite; a program needn't handle non-finite values.
Results may differ from a plain program's by a relative error of at most 0.028.
Values may be sent and summed in bfloat16 or wider, within the bound.
No kernel may reach another device: no remote copies, remote signals or barrier semaphores. Data moves between devices by JAX's collectives and lax.ppermute only.
A program may use at most 320 MiB of HBM per device.

v0:
```python
import math
import jax
import jax.numpy as jnp
from jax import lax
from jax.sharding import PartitionSpec as P

HEADS = 16
PROMPT = 1024
EPS = 1e-06
MU = 0.9
LOG2E = 1.442695041
NEG = -1e30
PRECISION_HIGH = lax.Precision.HIGHEST


def rms_scale(field):
    return lax.rsqrt(jnp.mean(field * field, axis=-1, keepdims=True) + EPS)


def norm_back(field, scale, gain_vec, grad_in):
    weighted = grad_in * gain_vec
    inner = jnp.mean(field * weighted, axis=-1, keepdims=True)
    return scale * weighted - field * (scale * scale * scale) * inner


def orthonormal(factor):
    columns = []
    for col_index in range(factor.shape[-1]):
        column = factor[..., col_index]
        for earlier in columns:
            column = column - jnp.sum(earlier * column, axis=-2, keepdims=True) * earlier
        column = column * lax.rsqrt(jnp.sum(column * column, axis=-2, keepdims=True) + EPS)
        columns.append(column)
    return jnp.stack(columns, axis=-1)


def on_device(
    tokens,
    cotangent,
    weights,
    vectors,
    error,
    previous_right_factors,
    momentum,
    vec_momentum,
    prompt_len,
):
    f32 = jnp.float32
    bf16 = jnp.bfloat16
    zero_index = lax.axis_index("zero")
    rep_index = lax.axis_index("rep")
    zero_count = lax.axis_size("zero")
    rep_count = lax.axis_size("rep")
    tok_rows, feat_width = tokens.shape
    head_dim = feat_width // HEADS
    prompt_rows = PROMPT // zero_count
    prompt_valid = prompt_len[0]
    full_w, full_v = (
        lax.all_gather(weights, "zero", axis=0, tiled=True),
        lax.all_gather(vectors, "zero", axis=1, tiled=True),
    )
    vec_float = full_v.astype(f32)
    gain_one = vec_float[0]
    gain_two = vec_float[1]
    bias_one = vec_float[2]
    bias_two = vec_float[3]
    scale_raw = vec_float[4]
    tok_float = tokens.astype(f32)
    scale_one = rms_scale(tok_float)
    normed_one = (tok_float * scale_one * gain_one).astype(bf16)
    projected = jnp.einsum("ti,omi->mto", normed_one, full_w[:, 0:3, :], preferred_element_type=f32)
    query = projected[0]
    key_low = projected[1].astype(bf16)
    value_low = projected[2].astype(bf16)
    scale_const = LOG2E / math.sqrt(head_dim)
    query_scale = scale_const * jax.nn.softplus(scale_raw)
    scaled = (query * query_scale).astype(bf16)
    key_far, value_far = (
        lax.all_gather(key_low[:prompt_rows], "zero", axis=0, tiled=True),
        lax.all_gather(value_low[:prompt_rows], "zero", axis=0, tiled=True),
    )
    key_rows = jnp.concatenate([key_far, key_low[prompt_rows:]], axis=0)
    value_rows = jnp.concatenate([value_far, value_low[prompt_rows:]], axis=0)
    key_count = key_rows.shape[0]
    q_row = lax.broadcasted_iota(jnp.int32, (tok_rows, key_count), 0)
    k_col = lax.broadcasted_iota(jnp.int32, (tok_rows, key_count), 1)
    q_prompt = q_row < prompt_rows
    q_pos = zero_index * prompt_rows + q_row
    k_prompt = k_col < PROMPT
    see_prompt = k_prompt & (k_col < prompt_valid) & (jnp.logical_not(q_prompt) | (k_col <= q_pos))
    see_cont = (
        jnp.logical_not(k_prompt)
        & jnp.logical_not(q_prompt)
        & (k_col - PROMPT <= q_row - prompt_rows)
    )
    allowed = see_prompt | see_cont
    q_heads = scaled.reshape(tok_rows, HEADS, head_dim)
    k_heads = key_rows.reshape(key_count, HEADS, head_dim)
    v_heads = value_rows.reshape(key_count, HEADS, head_dim)

    def masked_scores():
        raw_scores = jnp.einsum("thd,khd->htk", q_heads, k_heads, preferred_element_type=f32)
        return jnp.where(allowed[None], raw_scores, NEG)

    masked = masked_scores()
    row_top = jnp.max(masked, axis=-1, keepdims=True)
    log_total = row_top + jnp.log(jnp.sum(jnp.exp(masked - row_top), axis=-1, keepdims=True))
    probs = jnp.exp(masked - log_total)
    attended = (
        jnp.einsum("htk,khd->thd", probs.astype(bf16), v_heads, preferred_element_type=f32)
        .reshape(tok_rows, feat_width)
        .astype(bf16)
    )
    branch = jnp.einsum("ti,oi->to", attended, full_w[:, 3, :], preferred_element_type=f32)
    hidden = tok_float + branch
    scale_two = rms_scale(hidden)
    normed_two = (hidden * scale_two * gain_two).astype(bf16)
    upper = (
        jnp.einsum("ti,oi->to", normed_two, full_w[:, 4, :], preferred_element_type=f32) + bias_one
    )
    activ = jax.nn.silu(upper).astype(bf16)
    output = jnp.einsum("ti,oi->to", activ, full_w[:, 5, :], preferred_element_type=f32) + bias_two
    result = (hidden + output).astype(bf16)
    back_w = lax.all_gather(weights, "zero", axis=0, tiled=True)
    grad_out = cotangent.astype(f32)
    grad_f = grad_out.astype(bf16)
    grad_act = jnp.einsum("to,oi->ti", grad_f, back_w[:, 5, :], preferred_element_type=f32)
    gate_sig = jax.nn.sigmoid(upper)
    grad_up = (grad_act * gate_sig * (1.0 + upper * (1.0 - gate_sig))).astype(bf16)
    grad_n2 = jnp.einsum("to,oi->ti", grad_up, back_w[:, 4, :], preferred_element_type=f32)
    grad_gain_two = jnp.sum(grad_n2 * hidden * scale_two, axis=0)
    grad_hidden = grad_out + norm_back(hidden, scale_two, gain_two, grad_n2)
    grad_branch = grad_hidden.astype(bf16)
    grad_att = jnp.einsum(
        "to,oi->ti", grad_branch, back_w[:, 3, :], preferred_element_type=f32
    ).astype(bf16)
    grad_att_heads = grad_att.reshape(tok_rows, HEADS, head_dim)
    probs_again = jnp.exp(masked_scores() - log_total)
    grad_probs = jnp.einsum("thd,khd->htk", grad_att_heads, v_heads, preferred_element_type=f32)
    delta = jnp.sum(probs_again * grad_probs, axis=-1, keepdims=True)
    grad_scores = (probs_again * (grad_probs - delta)).astype(bf16)
    grad_values = jnp.einsum(
        "htk,thd->khd", probs_again.astype(bf16), grad_att_heads, preferred_element_type=f32
    ).reshape(key_count, feat_width)
    grad_keys = jnp.einsum(
        "htk,thd->khd", grad_scores, q_heads, preferred_element_type=f32
    ).reshape(key_count, feat_width)
    grad_sq = jnp.einsum("htk,khd->thd", grad_scores, k_heads, preferred_element_type=f32).reshape(
        tok_rows, feat_width
    )
    own_keys, own_values = (
        lax.psum_scatter(
            grad_keys[:PROMPT].astype(jnp.bfloat16), "zero", scatter_dimension=0, tiled=True
        ).astype(jnp.float32),
        lax.psum_scatter(
            grad_values[:PROMPT].astype(jnp.bfloat16), "zero", scatter_dimension=0, tiled=True
        ).astype(jnp.float32),
    )
    grad_key = jnp.concatenate([own_keys, grad_keys[PROMPT:]], axis=0).astype(bf16)
    grad_value = jnp.concatenate([own_values, grad_values[PROMPT:]], axis=0).astype(bf16)
    grad_query = (grad_sq * query_scale).astype(bf16)
    grad_scale_raw = jnp.sum(grad_sq * query, axis=0) * scale_const * jax.nn.sigmoid(scale_raw)
    grad_proj = jnp.stack([grad_query, grad_key, grad_value], axis=0)
    grad_n1 = jnp.einsum("mto,omi->ti", grad_proj, back_w[:, 0:3, :], preferred_element_type=f32)
    grad_gain_one = jnp.sum(grad_n1 * tok_float * scale_one, axis=0)
    grad_tokens = grad_hidden + norm_back(tok_float, scale_one, gain_one, grad_n1)
    grad_stack = jnp.stack([grad_query, grad_key, grad_value, grad_branch, grad_up, grad_f], axis=0)
    input_stack = jnp.stack(
        [normed_one, normed_one, normed_one, attended, normed_two, activ], axis=0
    )
    grad_block = lax.psum_scatter(
        jnp.einsum("mto,mti->omi", grad_stack, input_stack, preferred_element_type=f32).astype(
            jnp.bfloat16
        ),
        "zero",
        scatter_dimension=0,
        tiled=True,
    ).astype(jnp.float32)
    vec_terms = jnp.stack(
        [
            grad_gain_one,
            grad_gain_two,
            jnp.sum(grad_up.astype(f32), axis=0),
            jnp.sum(grad_f.astype(f32), axis=0),
            grad_scale_raw,
        ],
        axis=0,
    )
    vec_block = lax.psum_scatter(vec_terms, "zero", scatter_dimension=1, tiled=True)
    combined_result = grad_block + error
    local_left_factor = jnp.einsum(
        "edn,dnw->edw", combined_result, previous_right_factors, precision=PRECISION_HIGH
    )
    vec_total = lax.psum(vec_block, "rep")
    left_parts = []
    right_parts = []
    for mat_index in range(combined_result.shape[1]):
        left_sum = lax.psum(local_left_factor[:, mat_index], "rep")
        left_ortho = orthonormal(left_sum[:, None, :] / rep_count)[:, 0, :]
        right_term = jnp.einsum(
            "oi,or->ir", combined_result[:, mat_index], left_ortho, precision=PRECISION_HIGH
        )
        right_parts.append(lax.psum(right_term.astype(jnp.bfloat16), "rep").astype(jnp.float32))
        left_parts.append(left_ortho)
    orthogonalized = jnp.stack(left_parts, axis=1)
    right_total = jnp.stack(right_parts, axis=0)
    fresh_right_factors = right_total / rep_count
    approximation = jnp.einsum(
        "upt,pqt->upq", orthogonalized, fresh_right_factors, precision=PRECISION_HIGH
    )
    new_error = combined_result - approximation
    rep_width = feat_width // rep_count
    grad_weights = lax.dynamic_slice_in_dim(approximation, rep_index * rep_width, rep_width, 2)
    step_rate = 0.03 / math.sqrt(zero_count * tok_rows)
    new_momentum = MU * momentum + grad_weights
    update_weights = -step_rate * new_momentum
    grad_vectors = vec_total / rep_count
    new_vec_momentum = MU * vec_momentum + grad_vectors
    update_vectors = -step_rate * new_vec_momentum
    return (
        result,
        grad_tokens,
        grad_weights,
        grad_vectors,
        new_error,
        fresh_right_factors,
        new_momentum,
        new_vec_momentum,
        update_weights,
        update_vectors,
    )


def solution(mesh):
    in_specs = (
        P(("rep", "zero"), None),
        P(("rep", "zero"), None),
        P("zero", None, None),
        P(None, "zero"),
        P(("rep", "zero"), None, None),
        P(None, None, "zero"),
        P("zero", None, "rep"),
        P(None, "zero"),
        P("rep"),
    )
    out_specs = (
        P(("rep", "zero"), None),
        P(("rep", "zero"), None),
        P("zero", None, "rep"),
        P(None, "zero"),
        P(("rep", "zero"), None, None),
        P(None, None, "zero"),
        P("zero", None, "rep"),
        P(None, "zero"),
        P("zero", None, "rep"),
        P(None, "zero"),
    )
    return jax.shard_map(
        on_device, mesh=mesh, in_specs=in_specs, out_specs=out_specs, check_vma=False
    )
```

profile of v0, /device:TPU:0, one launch (start us, length us, event | category | flops | bytes accessed | tf_op | source)
XLA Modules:
  0.0 1215.3 jit_solution(3644075702543074997)
XLA Ops:
  15.9 120.7 %all-gather.7.cloned.1.call-done = bf16[1280,6,1280]{2,0,1:T(8,128)(2,1)} async-done(((bf16[320,6,1280]{2,0,1:T(8,128)(2,1)}), bf16[1280,6,1280]{2,0,1:T(8,128)(2,1)}) %all-gather.7.cloned.1.call-update) | async-done | bytes 19660816 | tf_op jit(solution)/shard_map/all_gather | solution.py:59
  163.3 12.1 all-gather.9.cloned.1.call-done
  175.4 27.7 %all-gather.11.cloned.1.call-done = bf16[1,1024,1280]{2,1,0:T(8,128)(2,1)} async-done(((bf16[1,256,1280]{2,1,0:T(8,128)(2,1)}), bf16[1,1024,1280]{2,1,0:T(8,128)(2,1)}) %all-gather.11.cloned.1.call-update) | async-done | bytes 2621456 | tf_op jit(solution)/shard_map/all_gather | solution.py:79
  218.6 13.1 %select_reduce_fusion = (f32[16,384]{1,0:T(8,128)S(1)}, f32[16,384,1152]{2,1,0:T(8,128)}) fusion(pred[384,1152]{1,0:T(8,128)(4,1)} %fusion.50, bf16[1152,16,80]{0,2,1:T(8,128)(2,1)} %bitcast.662, f32[384,16,80]{0,2,1:T(8,128)S(1)} %bitcast.659, f32[16,80]{1,0:T(8,128)S(1)} %mul.16566), kind=kOutput, calls=%fused_computation.5 | convolution fusion | flops 1147594752 | bytes 33698816 | tf_op jit(solution)/shard_map/thd,khd->htk/dot_general | solution.py:102
  231.6 13.7 %exponential_reduce_fusion = f32[16,384]{1,0:T(8,128)S(1)} fusion(f32[16,384,1152]{2,1,0:T(8,128)} %get-tuple-element.459, f32[16,384]{1,0:T(8,128)S(1)} %get-tuple-element.458, pred[384,1152]{1,0:T(8,128)(4,1)S(1)} %copy-done.3), kind=kLoop, calls=%fused_computation.3 | loop fusion | flops 21227520 | bytes 28803072 | tf_op jit(solution)/shard_map/reduce_sum | solution.py:107
  245.3 13.1 %fusion.51 = bf16[16,80,384]{2,1,0:T(8,128)(2,1)} fusion(bf16[1152,16,80]{0,2,1:T(8,128)(2,1)S(1)} %bitcast.665, f32[16,384,1152]{2,1,0:T(8,128)} %get-tuple-element.459, f32[16,384]{1,0:T(8,128)S(1)} %log_add_fusion, pred[384,1152]{1,0:T(8,128)(4,1)S(1)} %copy-done.3), kind=kOutput, calls=%fused_computation.96 | convolution fusion | flops 1154187264 | bytes 32710656 | tf_op jit(solution)/shard_map/htk,khd->thd/dot_general | solution.py:110
  289.8 24.5 %multiply_reduce_fusion = (f32[16,384]{1,0:T(8,128)S(1)}, f32[16,384,1152]{2,1,0:T(8,128)}) fusion(f32[16,384,1152]{2,1,0:T(8,128)} %get-tuple-element.459, f32[16,384]{1,0:T(8,128)S(1)} %log_add_fusion, pred[384,1152]{1,0:T(8,128)(4,1)} %fusion.50, bf16[384,16,80]{0,2,1:T(8,128)(2,1)} %bitcast.669, bf16[1152,16,80]{0,2,1:T(8,128)(2,1)} %bitcast.664), kind=kOutput, calls=%fused_computation.1 | convolution fusion | flops 1160767488 | bytes 61046784 | tf_op jit(solution)/shard_map/thd,khd->htk/dot_general | solution.py:139
  314.3 23.7 %multiply_convert_fusion = bf16[16,384,1152]{2,1,0:T(8,128)(2,1)} fusion(f32[16,384,1152]{2,1,0:T(8,128)} %get-tuple-element.464, f32[16,384,1152]{2,1,0:T(8,128)} %get-tuple-element.459, f32[16,384]{1,0:T(8,128)S(1)} %get-tuple-element.463, f32[16,384]{1,0:T(8,128)S(1)} %log_add_fusion, pred[384,1152]{1,0:T(8,128)(4,1)} %fusion.50), kind=kLoop, calls=%fused_computation | loop fusion | flops 35389440 | bytes 71270400 | tf_op jit(solution)/shard_map/convert_element_type | solution.py:141
  354.1 14.2 %fusion.9 = bf16[1152,16,80]{0,2,1:T(8,128)(2,1)S(1)} fusion(bf16[384,16,80]{0,2,1:T(8,128)(2,1)} %bitcast.670, f32[16,384,1152]{2,1,0:T(8,128)} %get-tuple-element.459, f32[16,384]{1,0:T(8,128)S(1)} %log_add_fusion, pred[384,1152]{1,0:T(8,128)(4,1)} %fusion.50), kind=kOutput, calls=%fused_computation.23 | convolution fusion | flops 1155170304 | bytes 32710656 | tf_op jit(solution)/shard_map/htk,thd->khd/dot_general | solution.py:142
  380.8 11.7 fusion.44
  401.2 24.4 %reduce-scatter.11.cloned.1.call-done = bf16[256,1280]{1,0:T(8,128)(2,1)} async-done(((bf16[1024,1280]{1,0:T(8,128)(2,1)}), bf16[256,1280]{1,0:T(8,128)(2,1)}) %reduce-scatter.11.cloned.1.call-update) | async-done | bytes 655376 | tf_op jit(solution)/shard_map/reduce_scatter | solution.py:155
  442.1 17.9 %convolution_convert_fusion = bf16[6,1280,1280]{2,1,0:T(8,128)(2,1)} fusion(bf16[6,384,1280]{2,1,0:T(8,128)(2,1)} %get-tuple-element.466, bf16[6,384,1280]{2,1,0:T(8,128)(2,1)} %bitcast_dynamic-update-slice_fusion), kind=kOutput, calls=%fused_computation.4 | convolution fusion | flops 7559577600 | bytes 31457280 | tf_op jit(solution)/shard_map/mto,mti->omi/dot_general | solution.py:172
  460.0 26.4 %copy.101 = bf16[1280,7680]{1,0:T(8,128)(2,1)} copy(bf16[1280,7680]{0,1:T(8,128)(2,1)} %bitcast.668) | data formatting | bytes 39321600
  497.8 131.3 %reduce-scatter.13.cloned.1.call-done = bf16[320,7680]{1,0:T(8,128)(2,1)} async-done(((bf16[1280,7680]{1,0:T(8,128)(2,1)}), bf16[320,7680]{1,0:T(8,128)(2,1)}) %reduce-scatter.13.cloned.1.call-update) | async-done | bytes 4915216
  656.0 10.7 convolution_bitcast_fusion
  671.0 68.0 %all-reduce.5.cloned.1.call-done = (f32[320,8]{0,1:T(8,128)}, f32[320,8]{0,1:T(8,128)}, f32[320,8]{0,1:T(8,128)}, f32[320,8]{0,1:T(8,128)}, f32[320,8]{0,1:T(8,128)}, /*index=5*/f32[320,8]{0,1:T(8,128)}, f32[5,320]{1,0:T(8,128)}) async-done(((f32[320,8]{0,1:T(8,128)}, f32[320,8]{0,1:T(8,128)}, f32[320,8]{0,1:T(8,128)}, f32[320,8]{0,1:T(8,128)}, f32[320,8]{0,1:T(8,128)}, /*index=5*/f32[320,8]{0,1:T(8,128)}, ...) | async-done | bytes 67856 | tf_op jit(solution)/shard_map/psum | solution.py:198
  780.5 17.7 %subtract_multiply_fusion.35 = (f32[320,1,1]{0,2,1:T(1,128)S(1)}, f32[320,1,1]{0,2,1:T(1,128)S(1)}, f32[320,1,1]{0,2,1:T(1,128)S(1)}, f32[320,1,1]{0,2,1:T(1,128...) fusion(f32[320,1,1]{0,2,1:T(1,128)S(1)} %get-tuple-element.437, ...), kind=kLoop, calls=%fused_computation.622 | loop fusion | flops 20160 | bytes 19340 | tf_op jit(solution)/shard_map/mul | solution.py:32
  842.7 17.6 %subtract_multiply_fusion.28 = (f32[320,1,1]{0,2,1:T(1,128)S(1)}, f32[320,1,1]{0,2,1:T(1,128)S(1)}, f32[320,1,1]{0,2,1:T(1,128)S(1)}, f32[320,1,1]{0,2,1:T(1,128...) fusion(f32[320,1,1]{0,2,1:T(1,128)S(1)} %get-tuple-element.404, ...), kind=kLoop, calls=%fused_computation.566 | loop fusion | flops 20160 | bytes 19340 | tf_op jit(solution)/shard_map/mul | solution.py:32
  904.0 17.6 %subtract_multiply_fusion.21 = (f32[320,1,1]{0,2,1:T(1,128)S(1)}, f32[320,1,1]{0,2,1:T(1,128)S(1)}, f32[320,1,1]{0,2,1:T(1,128)S(1)}, f32[320,1,1]{0,2,1:T(1,128...) fusion(f32[320,1,1]{0,2,1:T(1,128)S(1)} %get-tuple-element.371, ...), kind=kLoop, calls=%fused_computation.510 | loop fusion | flops 20160 | bytes 19340 | tf_op jit(solution)/shard_map/mul | solution.py:32
  965.4 17.6 %subtract_multiply_fusion.14 = (f32[320,1,1]{0,2,1:T(1,128)S(1)}, f32[320,1,1]{0,2,1:T(1,128)S(1)}, f32[320,1,1]{0,2,1:T(1,128)S(1)}, f32[320,1,1]{0,2,1:T(1,128...) fusion(f32[320,1,1]{0,2,1:T(1,128)S(1)} %get-tuple-element.338, ...), kind=kLoop, calls=%fused_computation.454 | loop fusion | flops 20160 | bytes 19340 | tf_op jit(solution)/shard_map/mul | solution.py:32
  1026.8 17.6 %subtract_multiply_fusion.7 = (f32[320,1,1]{0,2,1:T(1,128)S(1)}, f32[320,1,1]{0,2,1:T(1,128)S(1)}, f32[320,1,1]{0,2,1:T(1,128)S(1)}, f32[320,1,1]{0,2,1:T(1,128)...) fusion(f32[320,1,1]{0,2,1:T(1,128)S(1)} %get-tuple-element.305, ...), kind=kLoop, calls=%fused_computation.398 | loop fusion | flops 20160 | bytes 19340 | tf_op jit(solution)/shard_map/mul | solution.py:32
  1088.3 17.5 %subtract_multiply_fusion = (f32[320,1,1]{0,2,1:T(1,128)S(1)}, f32[320,1,1]{0,2,1:T(1,128)S(1)}, f32[320,1,1]{0,2,1:T(1,128)S(1)}, f32[320,1,1]{0,2,1:T(1,128)S(...) fusion(f32[320,1,1]{0,2,1:T(1,128)S(1)} %get-tuple-element.272, f32[]{:T(128)S(6)} %rsqrt.263, ...), kind=kLoop, calls=%fused_computation.342 | loop fusion | flops 20160 | bytes 19340 | tf_op jit(solution)/shard_map/mul | solution.py:32
  1109.5 71.6 %all-reduce.7.cloned.1.call-done = (bf16[1,1280,8]{1,2,0:T(8,128)(2,1)}, bf16[1,1280,8]{1,2,0:T(8,128)(2,1)}, bf16[1,1280,8]{1,2,0:T(8,128)(2,1)}, bf16[1,1280,8...) async-done(((bf16[1,1280,8]{1,2,0:T(8,128)(2,1)}, bf16[1,1280,8]{1,2,0:T(8,128)(2,1)}, bf16[1,1280,8]{1,2,0:T(8,128)(2,1)}, ...) | async-done | bytes 122896 | tf_op jit(solution)/shard_map/psum | solution.py:203
  1185.5 12.8 %bitcast_subtract_fusion = (f32[320,6,1280]{2,0,1:T(8,128)}, f32[6,1280,320]{1,2,0:T(8,128)S(1)}) fusion(f32[320,6,1280]{2,0,1:T(8,128)} %convert_add_fusion, f32[6,1280,8]{1,2,0:T(8,128)S(1)} %convert_multiply_fusion.5, f32[320,6,8]{0,2,1:T(8,128)S(1)} %constant_dynamic-update-slice_fusion.8), kind=kOutput, calls=%fused_computation.7 | convolution fusion | flops 238387200 | bytes 29798400 | tf_op jit(solution)/shard_map/upt,pqt->upq/dot_general | solution.py:208
  (304 shorter events, 424.6 us)
Async XLA Ops:
  7.2 648.8 %copy-start = (f32[6,1280,8]{1,2,0:T(8,128)S(1)}, f32[6,1280,8]{1,2,0:T(8,128)}, u32[]{:S(2)}) copy-start(f32[6,1280,8]{1,2,0:T(8,128)} %param.14) | copy-start | bytes 737284
  7.2 129.4 %all-gather.7.cloned.1.call-start = ((), (), s32[]{:S(2)}) async-start(), calls=%async_computation.4 | async-start | bytes 24576000 | tf_op jit(solution)/shard_map/all_gather | solution.py:59
  7.9 167.5 %all-gather.9.cloned.1.call-start = ((), (), s32[]{:S(2)}) async-start(), calls=%async_computation.7 | async-start | bytes 3276800 | tf_op jit(solution)/shard_map/all_gather | solution.py:80
  14.3 132.7 %copy-start.25 = (f32[1280,5]{0,1:T(8,128)}, f32[1280,5]{0,1:T(8,128)S(1)}, u32[]{:S(2)}) copy-start(f32[1280,5]{0,1:T(8,128)S(1)} %reshape.8102) | copy-start | bytes 76804
  15.0 136.4 %copy-start.26 = (f32[1280]{0:T(1024)}, f32[1280]{0:T(1024)S(1)}, u32[]{:S(2)}) copy-start(f32[1280]{0:T(1024)S(1)} %get-tuple-element.55) | copy-start | bytes 15364
  15.0 138.7 %copy-start.22 = (f32[1280]{0:T(1024)}, f32[1280]{0:T(1024)S(1)}, u32[]{:S(2)}) copy-start(f32[1280]{0:T(1024)S(1)} %get-tuple-element.58) | copy-start | bytes 15364
  15.8 137.9 %copy-start.28 = (f32[384]{0:T(512)}, f32[384]{0:T(512)S(1)}, u32[]{:S(2)}) copy-start(f32[384]{0:T(512)S(1)} %get-tuple-element.453) | copy-start | bytes 4612
  149.7 53.4 %all-gather.11.cloned.1.call-start = ((), (), s32[]{:S(2)}) async-start(), calls=%async_computation.8 | async-start | bytes 3276800 | tf_op jit(solution)/shard_map/all_gather | solution.py:79
  150.5 248.2 %reduce-scatter.9.cloned.1.call-start = ((), (), s32[]{:S(2)}) async-start(), calls=%async_computation.5 | async-start | bytes 3276800 | tf_op jit(solution)/shard_map/reduce_scatter | solution.py:152
  231.6 13.7 %copy-start.2 = (bf16[1152,1280]{0,1:T(8,128)(2,1)S(1)}, bf16[1152,1280]{0,1:T(8,128)(2,1)}, u32[]{:S(2)}) copy-start(bf16[1152,1280]{0,1:T(8,128)(2,1)} %copy.80) | copy-start | bytes 8847364
  264.9 16.4 %copy-start.9 = (f32[384,1280]{1,0:T(8,128)}, f32[384,1280]{1,0:T(8,128)S(1)}, u32[]{:S(2)}) copy-start(f32[384,1280]{1,0:T(8,128)S(1)} %get-tuple-element.461) | copy-start | bytes 5898244
  354.0 71.6 %reduce-scatter.11.cloned.1.call-start = ((), (), s32[]{:S(2)}) async-start(), calls=%async_computation.6 | async-start | bytes 3276800 | tf_op jit(solution)/shard_map/reduce_scatter | solution.py:155
  376.2 119.9 %reduce-scatter.15.cloned.1.call-start = ((), (), s32[]{:S(2)}) async-start(), calls=%async_computation.10 | async-start | bytes 819200
  397.3 28.3 %copy-start.14 = (bf16[1,128,1280]{2,1,0:T(8,128)(2,1)S(1)}, bf16[1,128,1280]{2,1,0:T(8,128)(2,1)}, u32[]{:S(2)}) copy-start(bf16[1,128,1280]{2,1,0:T(8,128)(2,1)} %copy.88) | copy-start | bytes 983044
  398.7 29.2 %copy-start.6 = (f32[384,1280]{1,0:T(8,128)S(1)}, f32[384,1280]{1,0:T(8,128)}, u32[]{:S(2)}) copy-start(f32[384,1280]{1,0:T(8,128)} %copy-done.5) | copy-start | bytes 5898244
  442.1 187.0 %reduce-scatter.13.cloned.1.call-start = ((), (), s32[]{:S(2)}) async-start(), calls=%async_computation.9 | async-start | bytes 24576000
  486.4 252.5 %all-reduce.5.cloned.1.call-start = ((), (), s32[]{:S(2)}) async-start(), calls=%async_computation.11 | async-start | bytes 172032 | tf_op jit(solution)/shard_map/psum | solution.py:198
  667.3 513.8 %all-reduce.7.cloned.1.call-start = ((), (), s32[]{:S(2)}) async-start(), calls=%async_computation.12 | async-start | bytes 245760 | tf_op jit(solution)/shard_map/psum | solution.py:203
  739.0 124.4 %copy-start.34 = (f32[320,8]{0,1:T(8,128)S(1)}, f32[320,8]{0,1:T(8,128)}, u32[]{:S(2)}) copy-start(f32[320,8]{0,1:T(8,128)} %get-tuple-element.223) | copy-start | bytes 30724
  798.1 126.5 %copy-start.33 = (f32[320,8]{0,1:T(8,128)S(1)}, f32[320,8]{0,1:T(8,128)}, u32[]{:S(2)}) copy-start(f32[320,8]{0,1:T(8,128)} %get-tuple-element.224) | copy-start | bytes 30724
  860.3 125.8 %copy-start.32 = (f32[320,8]{0,1:T(8,128)S(1)}, f32[320,8]{0,1:T(8,128)}, u32[]{:S(2)}) copy-start(f32[320,8]{0,1:T(8,128)} %get-tuple-element.225) | copy-start | bytes 30724
  921.6 125.8 %copy-start.31 = (f32[320,8]{0,1:T(8,128)S(1)}, f32[320,8]{0,1:T(8,128)}, u32[]{:S(2)}) copy-start(f32[320,8]{0,1:T(8,128)} %get-tuple-element.226) | copy-start | bytes 30724
  983.0 125.8 %copy-start.35 = (f32[5,320]{1,0:T(8,128)S(1)}, f32[5,320]{1,0:T(8,128)}, u32[]{:S(2)}) copy-start(f32[5,320]{1,0:T(8,128)} %param.16) | copy-start | bytes 19204
  983.1 125.8 %copy-start.36 = (f32[5,320]{1,0:T(8,128)S(1)}, f32[5,320]{1,0:T(8,128)}, u32[]{:S(2)}) copy-start(f32[5,320]{1,0:T(8,128)} %get-tuple-element.227) | copy-start | bytes 19204
  (29 other events, 137.0 us)
Sparse Core Ops, SparseCore 0:
  9.6 126.9 all-gather.6
  149.9 25.5 all-gather.8
  177.6 25.5 all-gather.10
  354.1 34.4 reduce-scatter.8
  391.1 34.5 reduce-scatter.10
  442.2 22.4 reduce-scatter.14
  486.6 142.4 reduce-scatter.12
  667.5 71.4 all-reduce.4
  1109.6 71.4 all-reduce.6
where the time goes:
time: 1230 us; the launch traced here: 1220 us
  waiting for transfers between devices  457 us (37%)
  other arithmetic  393 us (32%)
  matrix products  192 us (16%)
  local copies, waits for them, and re-layouts  118 us (10%)
  between operations  47.3 us (4%)
    reduce_sum x60, other arithmetic, orthonormal(): jnp.sum(earlier * column, axis=-2, keepdims=True) * earlier  164 us
    unnamed x11, waiting for transfers between devices  133 us
    all_gather x1, waiting for transfers between devices, on_device(): lax.all_gather(weights, 'zero', axis=0, tiled=True)  121 us
    mul x6, other arithmetic, orthonormal(): column * lax.rsqrt(jnp.sum(column * column, axis=-2, keepdims=True) + EPS)  106 us
    psum x1, waiting for transfers between devices, on_device(): lax.psum(right_term.astype(jnp.bfloat16), 'rep').astype(jnp.float32)  71.6 us
    psum x1, waiting for transfers between devices, on_device(): left_sum = lax.psum(local_left_factor[:, mat_index], 'rep')  68 us
    unnamed x106, local copies, waits for them, and re-layouts  62 us
    reduce_sum x30, other arithmetic, orthonormal(): jnp.sum(column * column, axis=-2, keepdims=True) + EPS  49.2 us
  transfers between devices with their start and end apart: 9, of which 7 were waited for; matrix products, arithmetic and copies ran while one was open for 9% of the time, Pallas kernels for 0%

commit v1 on v0

--- a/solution.py
+++ b/solution.py
@@ -11,6 +11,31 @@
 LOG2E = 1.442695041
 NEG = -1e30
 PRECISION_HIGH = lax.Precision.HIGHEST
+
+
+def fix_axis_part(mat, dim_i):
+    mat = jnp.moveaxis(mat, 0, dim_i)
+    v_now = mat.shape
+    return mat.reshape(*v_now[:dim_i], v_now[dim_i] * v_now[dim_i + 1], *v_now[dim_i + 2 :])
+
+
+def units_save(axis_no, x_local, bus_axis):
+    nd = lax.axis_size(bus_axis)
+    gallery = [(nth, (nth + 1) % nd) for nth in range(nd)]
+    windows = [(pp, it) for it, pp in gallery]
+    x_now, item_now = ([], [])
+    for b in range(nd - 1):
+        if b % 2 == 0:
+            passed = lax.ppermute(x_now[-1] if x_now else x_local, bus_axis, gallery)
+            x_now.append(passed)
+        else:
+            item_now.append(lax.ppermute(item_now[-1] if item_now else x_local, bus_axis, windows))
+    reply = jnp.stack([*x_now[::-1], x_local, *item_now], axis=0)
+    carry = lax.axis_index(bus_axis)
+    small = len(x_now)
+    outcome_arr = carry - small
+    reply = reply[(jnp.arange(nd) - outcome_arr) % nd]
+    return fix_axis_part(reply, axis_no)
 
 
 def rms_scale(field):
@@ -56,7 +81,7 @@
     prompt_rows = PROMPT // zero_count
     prompt_valid = prompt_len[0]
     full_w, full_v = (
-        lax.all_gather(weights, "zero", axis=0, tiled=True),
+        units_save(0, weights, "zero"),
         lax.all_gather(vectors, "zero", axis=1, tiled=True),
     )
     vec_float = full_v.astype(f32)

time: 1230 us -> 1380 us (1.12)
  waiting for transfers between devices: 457 us -> 510 us
  blocking collectives: 6.25 us -> 54.4 us
  other arithmetic: 393 us -> 418 us
  local copies, waits for them, and re-layouts: 118 us -> 137 us
    ppermute x0 -> x3, waiting for transfers between devices: none -> 104 us  [the longest x2 104 us: units_save(): passed = lax.ppermute(x_now[-1] if x_now else x_local, bus_axis, gallery)]
    all_gather x1, blocking collectives: 6.25 us -> 54.4 us  [on_device(): lax.all_gather(vectors, 'zero', axis=1, tiled=True)]
    all_gather x1, waiting for transfers between devices: 121 us -> 92.3 us  [on_device(): back_w = lax.all_gather(weights, 'zero', axis=0, tiled=True)]
    gather x0 -> x4, local copies, waits for them, and re-layouts: none -> 26.2 us  [units_save(): reply = reply[(jnp.arange(nd) - outcome_arr) % nd]]
    unnamed x106 -> x117, local copies, waits for them, and re-layouts: 62 us -> 67.9 us
  transfers between devices with their start and end apart: 9 -> 12, of which waited for: 7 -> 8; matrix products, arithmetic and copies ran while one was open for 9% -> 13% of each run, Pallas kernels for 0% -> 0%
where the time goes in v1:
time: 1380 us; the launch traced here: 1370 us
  waiting for transfers between devices  510 us (37%)
  other arithmetic  418 us (30%)
  matrix products  196 us (14%)
  local copies, waits for them, and re-layouts  137 us (10%)
  blocking collectives  54.4 us (4%)
  between operations  47.1 us (3%)
    reduce_sum x60, other arithmetic, orthonormal(): jnp.sum(earlier * column, axis=-2, keepdims=True) * earlier  164 us
    unnamed x11, waiting for transfers between devices  133 us
    mul x6, other arithmetic, orthonormal(): column * lax.rsqrt(jnp.sum(column * column, axis=-2, keepdims=True) + EPS)  106 us
    ppermute x2, waiting for transfers between devices, units_save(): passed = lax.ppermute(x_now[-1] if x_now else x_local, bus_axis, gallery)  104 us
    all_gather x1, waiting for transfers between devices, on_device(): back_w = lax.all_gather(weights, 'zero', axis=0, tiled=True)  92.3 us
    psum x1, waiting for transfers between devices, on_device(): lax.psum(right_term.astype(jnp.bfloat16), 'rep').astype(jnp.float32)  71.6 us
    psum x1, waiting for transfers between devices, on_device(): left_sum = lax.psum(local_left_factor[:, mat_index], 'rep')  68 us
    unnamed x117, local copies, waits for them, and re-layouts  67.9 us
  transfers between devices with their start and end apart: 12, of which 8 were waited for; matrix products, arithmetic and copies ran while one was open for 13% of the time, Pallas kernels for 0%

profile of v1, /device:TPU:0, one launch (start us, length us, event | category | flops | bytes accessed | tf_op | source)
XLA Modules:
  0.0 1369.3 jit_solution(4995776968461002093)
XLA Ops:
  9.8 104.2 %collective-permute-done = bf16[320,6,1280]{2,0,1:T(8,128)(2,1)} collective-permute-done((bf16[320,6,1280]{2,0,1:T(8,128)(2,1)}, bf16[320,6,1280]{2,0,1:T(8,128)(2,1)}, u32[]{:S(2)}, u32[]{:S(2)}) %collective-permute-start) | collective-permute-done | bytes 4915232 | tf_op jit(solution)/shard_map/ppermute | solution.py:29
  116.4 54.4 %all-gather.2 = bf16[4,320,5]{1,2,0:T(8,128)(2,1)S(1)} all-gather(bf16[1,320,5]{1,2,0:T(8,128)(2,1)} %bitcast.721), channel_id=1, replica_groups=mesh['rep'=8,'zero'=4] {'zero'}, dimensions={0}, use_global_device_ids=true | all-gather | bytes 16000 | tf_op jit(solution)/shard_map/all_gather | solution.py:85
  253.1 18.4 %all-gather.11.cloned.1.call-done = bf16[1,1024,1280]{1,2,0:T(8,128)(2,1)} async-done(((bf16[1,256,1280]{1,2,0:T(8,128)(2,1)}), bf16[1,1024,1280]{1,2,0:T(8,128)(2,1)}) %all-gather.11.cloned.1.call-update) | async-done | bytes 2621456 | tf_op jit(solution)/shard_map/all_gather | solution.py:104
  273.7 12.2 select_reduce_fusion
  285.8 13.5 exponential_reduce_fusion
  301.6 17.5 %fusion.53 = bf16[16,80,384]{2,1,0:T(8,128)(2,1)} fusion(bf16[1152,16,80]{0,2,1:T(8,128)(2,1)S(1)} %bitcast.694, f32[16,384,1152]{2,1,0:T(8,128)} %get-tuple-element.461, f32[16,384]{1,0:T(8,128)S(1)} %log_add_fusion, pred[384,1152]{1,0:T(8,128)(4,1)S(1)} %copy-done.5), kind=kOutput, calls=%fused_computation.107 | convolution fusion | flops 1154187264 | bytes 32710656 | tf_op jit(solution)/shard_map/htk,khd->thd/dot_general | solution.py:135
  333.0 92.3 %all-gather.7.cloned.1.call-done = bf16[1280,6,1280]{2,0,1:T(8,128)(2,1)} async-done(((bf16[320,6,1280]{2,0,1:T(8,128)(2,1)}), bf16[1280,6,1280]{2,0,1:T(8,128)(2,1)}) %all-gather.7.cloned.1.call-update) | async-done | bytes 19660816 | tf_op jit(solution)/shard_map/all_gather | solution.py:149
  444.3 24.5 %multiply_reduce_fusion = (f32[16,384]{1,0:T(8,128)S(1)}, f32[16,384,1152]{2,1,0:T(8,128)}) fusion(f32[16,384,1152]{2,1,0:T(8,128)} %get-tuple-element.461, f32[16,384]{1,0:T(8,128)S(1)} %log_add_fusion, pred[384,1152]{1,0:T(8,128)(4,1)} %fusion.52, bf16[384,16,80]{0,2,1:T(8,128)(2,1)} %bitcast.703, bf16[1152,16,80]{0,2,1:T(8,128)(2,1)} %bitcast.695), kind=kOutput, calls=%fused_computation.4 | convolution fusion | flops 1160767488 | bytes 61046784 | tf_op jit(solution)/shard_map/thd,khd->htk/dot_general | solution.py:164
  468.8 23.5 %multiply_convert_fusion = bf16[16,384,1152]{2,1,0:T(8,128)(2,1)} fusion(f32[16,384,1152]{2,1,0:T(8,128)} %get-tuple-element.466, f32[16,384,1152]{2,1,0:T(8,128)} %get-tuple-element.461, f32[16,384]{1,0:T(8,128)S(1)} %get-tuple-element.465, f32[16,384]{1,0:T(8,128)S(1)} %log_add_fusion, pred[384,1152]{1,0:T(8,128)(4,1)} %fusion.52), kind=kLoop, calls=%fused_computation.3 | loop fusion | flops 35389440 | bytes 71270400 | tf_op jit(solution)/shard_map/convert_element_type | solution.py:166
  508.4 14.2 %fusion.4 = bf16[1152,16,80]{0,2,1:T(8,128)(2,1)S(1)} fusion(bf16[384,16,80]{0,2,1:T(8,128)(2,1)} %bitcast.704, f32[16,384,1152]{2,1,0:T(8,128)} %get-tuple-element.461, f32[16,384]{1,0:T(8,128)S(1)} %log_add_fusion, pred[384,1152]{1,0:T(8,128)(4,1)} %fusion.52), kind=kOutput, calls=%fused_computation.27 | convolution fusion | flops 1155170304 | bytes 32710656 | tf_op jit(solution)/shard_map/htk,thd->khd/dot_general | solution.py:167
  534.3 11.7 fusion.46
  557.1 22.9 %reduce-scatter.11.cloned.1.call-done = bf16[256,1280]{1,0:T(8,128)(2,1)} async-done(((bf16[1024,1280]{1,0:T(8,128)(2,1)}), bf16[256,1280]{1,0:T(8,128)(2,1)}) %reduce-scatter.11.cloned.1.call-update) | async-done | bytes 655376 | tf_op jit(solution)/shard_map/reduce_scatter | solution.py:180
  596.4 17.9 %convolution_convert_fusion = bf16[6,1280,1280]{2,1,0:T(8,128)(2,1)} fusion(bf16[6,384,1280]{2,1,0:T(8,128)(2,1)} %get-tuple-element.468, bf16[6,384,1280]{2,1,0:T(8,128)(2,1)} %bitcast_dynamic-update-slice_fusion), kind=kOutput, calls=%fused_computation.7 | convolution fusion | flops 7559577600 | bytes 31457280 | tf_op jit(solution)/shard_map/mto,mti->omi/dot_general | solution.py:197
  614.3 26.4 %copy.90 = bf16[1280,7680]{1,0:T(8,128)(2,1)} copy(bf16[1280,7680]{0,1:T(8,128)(2,1)} %bitcast.702) | data formatting | bytes 39321600
  651.9 131.4 %reduce-scatter.13.cloned.1.call-done = bf16[320,7680]{1,0:T(8,128)(2,1)} async-done(((bf16[1280,7680]{1,0:T(8,128)(2,1)}), bf16[320,7680]{1,0:T(8,128)(2,1)}) %reduce-scatter.13.cloned.1.call-update) | async-done | bytes 4915216
  825.2 68.0 %all-reduce.5.cloned.1.call-done = (f32[320,8]{0,1:T(8,128)}, f32[320,8]{0,1:T(8,128)}, f32[320,8]{0,1:T(8,128)}, f32[320,8]{0,1:T(8,128)}, f32[320,8]{0,1:T(8,128)}, /*index=5*/f32[320,8]{0,1:T(8,128)}, f32[5,320]{1,0:T(8,128)}) async-done(((f32[320,8]{0,1:T(8,128)}, f32[320,8]{0,1:T(8,128)}, f32[320,8]{0,1:T(8,128)}, f32[320,8]{0,1:T(8,128)}, f32[320,8]{0,1:T(8,128)}, /*index=5*/f32[320,8]{0,1:T(8,128)}, ...) | async-done | bytes 67856 | tf_op jit(solution)/shard_map/psum | solution.py:223
  934.8 17.7 %subtract_multiply_fusion.35 = (f32[320,1,1]{0,2,1:T(1,128)S(1)}, f32[320,1,1]{0,2,1:T(1,128)S(1)}, f32[320,1,1]{0,2,1:T(1,128)S(1)}, f32[320,1,1]{0,2,1:T(1,128...) fusion(f32[320,1,1]{0,2,1:T(1,128)S(1)} %get-tuple-element.437, ...), kind=kLoop, calls=%fused_computation.638 | loop fusion | flops 20160 | bytes 19340 | tf_op jit(solution)/shard_map/mul | solution.py:57
  997.0 17.6 %subtract_multiply_fusion.28 = (f32[320,1,1]{0,2,1:T(1,128)S(1)}, f32[320,1,1]{0,2,1:T(1,128)S(1)}, f32[320,1,1]{0,2,1:T(1,128)S(1)}, f32[320,1,1]{0,2,1:T(1,128...) fusion(f32[320,1,1]{0,2,1:T(1,128)S(1)} %get-tuple-element.404, ...), kind=kLoop, calls=%fused_computation.582 | loop fusion | flops 20160 | bytes 19340 | tf_op jit(solution)/shard_map/mul | solution.py:57
  1058.3 17.6 %subtract_multiply_fusion.21 = (f32[320,1,1]{0,2,1:T(1,128)S(1)}, f32[320,1,1]{0,2,1:T(1,128)S(1)}, f32[320,1,1]{0,2,1:T(1,128)S(1)}, f32[320,1,1]{0,2,1:T(1,128...) fusion(f32[320,1,1]{0,2,1:T(1,128)S(1)} %get-tuple-element.371, ...), kind=kLoop, calls=%fused_computation.526 | loop fusion | flops 20160 | bytes 19340 | tf_op jit(solution)/shard_map/mul | solution.py:57
  1119.7 17.6 %subtract_multiply_fusion.14 = (f32[320,1,1]{0,2,1:T(1,128)S(1)}, f32[320,1,1]{0,2,1:T(1,128)S(1)}, f32[320,1,1]{0,2,1:T(1,128)S(1)}, f32[320,1,1]{0,2,1:T(1,128...) fusion(f32[320,1,1]{0,2,1:T(1,128)S(1)} %get-tuple-element.338, ...), kind=kLoop, calls=%fused_computation.470 | loop fusion | flops 20160 | bytes 19340 | tf_op jit(solution)/shard_map/mul | solution.py:57
  1181.1 17.6 %subtract_multiply_fusion.7 = (f32[320,1,1]{0,2,1:T(1,128)S(1)}, f32[320,1,1]{0,2,1:T(1,128)S(1)}, f32[320,1,1]{0,2,1:T(1,128)S(1)}, f32[320,1,1]{0,2,1:T(1,128)...) fusion(f32[320,1,1]{0,2,1:T(1,128)S(1)} %get-tuple-element.305, ...), kind=kLoop, calls=%fused_computation.414 | loop fusion | flops 20160 | bytes 19340 | tf_op jit(solution)/shard_map/mul | solution.py:57
  1242.6 17.5 %subtract_multiply_fusion = (f32[320,1,1]{0,2,1:T(1,128)S(1)}, f32[320,1,1]{0,2,1:T(1,128)S(1)}, f32[320,1,1]{0,2,1:T(1,128)S(1)}, f32[320,1,1]{0,2,1:T(1,128)S(...) fusion(f32[320,1,1]{0,2,1:T(1,128)S(1)} %get-tuple-element.272, f32[]{:T(128)S(6)} %rsqrt.263, ...), kind=kLoop, calls=%fused_computation.358 | loop fusion | flops 20160 | bytes 19340 | tf_op jit(solution)/shard_map/mul | solution.py:57
  1263.8 71.6 %all-reduce.7.cloned.1.call-done = (bf16[1,1280,8]{1,2,0:T(8,128)(2,1)}, bf16[1,1280,8]{1,2,0:T(8,128)(2,1)}, bf16[1,1280,8]{1,2,0:T(8,128)(2,1)}, bf16[1,1280,8...) async-done(((bf16[1,1280,8]{1,2,0:T(8,128)(2,1)}, bf16[1,1280,8]{1,2,0:T(8,128)(2,1)}, bf16[1,1280,8]{1,2,0:T(8,128)(2,1)}, ...) | async-done | bytes 122896 | tf_op jit(solution)/shard_map/psum | solution.py:228
  1339.8 12.8 bitcast_subtract_fusion
  (329 shorter events, 479.1 us)
Async XLA Ops:
  7.2 803.1 %copy-start = (f32[6,1280,8]{1,2,0:T(8,128)S(1)}, f32[6,1280,8]{1,2,0:T(8,128)}, u32[]{:S(2)}) copy-start(f32[6,1280,8]{1,2,0:T(8,128)} %param.14) | copy-start | bytes 737284
  7.2 264.3 %all-gather.11.cloned.1.call-start = ((), (), s32[]{:S(2)}) async-start(), calls=%async_computation.8 | async-start | bytes 3276800 | tf_op jit(solution)/shard_map/all_gather | solution.py:104
  7.2 106.8 %collective-permute-start = (bf16[320,6,1280]{2,0,1:T(8,128)(2,1)}, bf16[320,6,1280]{2,0,1:T(8,128)(2,1)}, u32[]{:S(2)}, u32[]{:S(2)}) collective-permute-start(bf16[320,6,1280]{2,0,1:T(8,128)(2,1)} %param.11), channel_id=1, source_target_pairs={{0,1},{1,2},{2,3},{3,0},{4,5},{5,6},{6,7},{7,4},{8,9},{9,10},{10,1... | collective-permute-start | bytes 14745608 | tf_op jit(solution)/shard_map/ppermute | solution.py:29
  7.8 166.1 %collective-permute-start.2 = (bf16[320,6,1280]{2,0,1:T(8,128)(2,1)}, bf16[320,6,1280]{2,0,1:T(8,128)(2,1)}, u32[]{:S(2)}, u32[]{:S(2)}) collective-permute-start(bf16[320,6,1280]{2,0,1:T(8,128)(2,1)} %param.11), channel_id=1, source_target_pairs={{1,0},{2,1},{3,2},{0,3},{5,4},{6,5},{7,6},{4,7},{9,8},{10,9},{11,1... | collective-permute-start | bytes 14745608 | tf_op jit(solution)/shard_map/ppermute | solution.py:32
  114.0 59.9 %collective-permute-start.1 = (bf16[320,6,1280]{2,0,1:T(8,128)(2,1)}, bf16[320,6,1280]{2,0,1:T(8,128)(2,1)}, u32[]{:S(2)}, u32[]{:S(2)}) collective-permute-start(bf16[320,6,1280]{2,0,1:T(8,128)(2,1)} %collective-permute-done), channel_id=1, source_target_pairs={{0,1},{1,2},{2,3},{3,0},{4,5},{5,6},{6,7},{7,4},{8,9},{9,10},{10,1... | collective-permute-start | bytes 14745608 | tf_op jit(solution)/shard_map/ppermute | solution.py:29
  171.7 72.7 %copy-start.30 = (f32[1280]{0:T(1024)}, f32[1280]{0:T(1024)S(1)}, u32[]{:S(2)}) copy-start(f32[1280]{0:T(1024)S(1)} %get-tuple-element.55) | copy-start | bytes 15364
  171.7 75.0 %copy-start.25 = (f32[1280]{0:T(1024)}, f32[1280]{0:T(1024)S(1)}, u32[]{:S(2)}) copy-start(f32[1280]{0:T(1024)S(1)} %get-tuple-element.58) | copy-start | bytes 15364
  173.9 72.8 %copy-start.32 = (f32[384]{0:T(512)}, f32[384]{0:T(512)S(1)}, u32[]{:S(2)}) copy-start(f32[384]{0:T(512)S(1)} %get-tuple-element.455) | copy-start | bytes 4612
  241.6 57.8 %all-gather.9.cloned.1.call-start = ((), (), s32[]{:S(2)}) async-start(), calls=%async_computation.7 | async-start | bytes 3276800 | tf_op jit(solution)/shard_map/all_gather | solution.py:105
  242.4 182.9 %all-gather.7.cloned.1.call-start = ((), (), s32[]{:S(2)}) async-start(), calls=%async_computation.4 | async-start | bytes 24576000 | tf_op jit(solution)/shard_map/all_gather | solution.py:149
  243.1 311.7 %reduce-scatter.9.cloned.1.call-start = ((), (), s32[]{:S(2)}) async-start(), calls=%async_computation.5 | async-start | bytes 3276800 | tf_op jit(solution)/shard_map/reduce_scatter | solution.py:177
  508.4 71.6 %reduce-scatter.11.cloned.1.call-start = ((), (), s32[]{:S(2)}) async-start(), calls=%async_computation.6 | async-start | bytes 3276800 | tf_op jit(solution)/shard_map/reduce_scatter | solution.py:180
  529.7 120.5 %reduce-scatter.15.cloned.1.call-start = ((), (), s32[]{:S(2)}) async-start(), calls=%async_computation.10 | async-start | bytes 819200
  549.3 30.6 %copy-start.17 = (bf16[1,128,1280]{2,1,0:T(8,128)(2,1)S(1)}, bf16[1,128,1280]{2,1,0:T(8,128)(2,1)}, u32[]{:S(2)}) copy-start(bf16[1,128,1280]{2,1,0:T(8,128)(2,1)} %copy.77) | copy-start | bytes 983044
  551.4 30.7 %copy-start.8 = (f32[384,1280]{1,0:T(8,128)S(1)}, f32[384,1280]{1,0:T(8,128)}, u32[]{:S(2)}) copy-start(f32[384,1280]{1,0:T(8,128)} %copy-done.7) | copy-start | bytes 5898244
  596.4 187.0 %reduce-scatter.13.cloned.1.call-start = ((), (), s32[]{:S(2)}) async-start(), calls=%async_computation.9 | async-start | bytes 24576000
  640.7 252.5 %all-reduce.5.cloned.1.call-start = ((), (), s32[]{:S(2)}) async-start(), calls=%async_computation.11 | async-start | bytes 172032 | tf_op jit(solution)/shard_map/psum | solution.py:223
  821.6 513.8 %all-reduce.7.cloned.1.call-start = ((), (), s32[]{:S(2)}) async-start(), calls=%async_computation.12 | async-start | bytes 245760 | tf_op jit(solution)/shard_map/psum | solution.py:228
  893.3 124.4 %copy-start.38 = (f32[320,8]{0,1:T(8,128)S(1)}, f32[320,8]{0,1:T(8,128)}, u32[]{:S(2)}) copy-start(f32[320,8]{0,1:T(8,128)} %get-tuple-element.223) | copy-start | bytes 30724
  893.3 185.7 %copy-start.37 = (f32[320,8]{0,1:T(8,128)S(1)}, f32[320,8]{0,1:T(8,128)}, u32[]{:S(2)}) copy-start(f32[320,8]{0,1:T(8,128)} %get-tuple-element.224) | copy-start | bytes 30724
  952.5 187.9 %copy-start.36 = (f32[320,8]{0,1:T(8,128)S(1)}, f32[320,8]{0,1:T(8,128)}, u32[]{:S(2)}) copy-start(f32[320,8]{0,1:T(8,128)} %get-tuple-element.225) | copy-start | bytes 30724
  1014.7 187.1 %copy-start.35 = (f32[320,8]{0,1:T(8,128)S(1)}, f32[320,8]{0,1:T(8,128)}, u32[]{:S(2)}) copy-start(f32[320,8]{0,1:T(8,128)} %get-tuple-element.226) | copy-start | bytes 30724
  1075.9 187.2 %copy-start.39 = (f32[5,320]{1,0:T(8,128)S(1)}, f32[5,320]{1,0:T(8,128)}, u32[]{:S(2)}) copy-start(f32[5,320]{1,0:T(8,128)} %param.16) | copy-start | bytes 19204
  1076.0 187.2 %copy-start.40 = (f32[5,320]{1,0:T(8,128)S(1)}, f32[5,320]{1,0:T(8,128)}, u32[]{:S(2)}) copy-start(f32[5,320]{1,0:T(8,128)} %get-tuple-element.227) | copy-start | bytes 19204
  (37 other events, 185.4 us)
Sparse Core Ops, SparseCore 0:
  241.8 29.6 all-gather.10
  273.6 25.8 all-gather.8
  301.1 124.2 all-gather.6
  508.5 34.4 reduce-scatter.8
  545.4 34.4 reduce-scatter.10
  596.5 22.4 reduce-scatter.14
  640.8 142.4 reduce-scatter.12
  821.8 71.4 all-reduce.4
  1263.9 71.4 all-reduce.6
